TPU v7x, 32 devices: a whole 2x2x4 slice. The times are simulated.
32 devices in a mesh: cand: 4 (over y, core), hid: 8 (over z, x).
Axes of the slice: x: 2, y: 2, z: 4, core: 2. Of those that a mesh axis runs over, the one named last changes fastest.
Arguments:
- tokens: bfloat16 [4, 256, 2048], P('cand', None, 'hid'), may hold values from -6 to 6
- cotangent: bfloat16 [4, 256, 2048], P('cand', None, 'hid'), may hold values from -6 to 6
- gate_weight: bfloat16 [2048, 8192], P('cand', 'hid'), may hold values from -0.125 to 0.125
- up_weight: bfloat16 [2048, 8192], P('cand', 'hid'), may hold values from -0.125 to 0.125
- down_weight: bfloat16 [8192, 2048], P('hid', 'cand'), may hold values from -0.125 to 0.125
- width_steps: int32 [4], P('cand'), may hold values from 1 to 8
- block_order: int32 [8], replicated, may hold values from 0 to 7, each once
Outputs:
- grad_tokens: float32 [4, 256, 2048], P('cand', None, 'hid')
- grad_gate: float32 [2048, 8192], P('cand', 'hid')
- grad_up: float32 [2048, 8192], P('cand', 'hid')
- grad_down: float32 [8192, 2048], P('hid', 'cand')
Inputs may be any that keep to these rules, and one draw needn't show every extreme that they name: Candidate c uses the first width_steps[c] * 1024 logical hidden units. `block_order`: names each of the 8 logical blocks once.
All inputs are finite; a program needn't handle non-finite values.
Results may differ from a plain program's by a relative error of at most 0.02.
Values may be sent and summed in bfloat16 or wider, within the bound.
A program may use at most 64 MiB of HBM per device.

v0:
```python
import jax
import jax.numpy as jnp
from jax import lax
from jax.sharding import PartitionSpec as P

FF = 8192


def shards(tokens, cotangent, gate_weight, up_weight, down_weight, width_steps, block_order):
    inputs, upstream = (
        lax.all_gather(tokens, "hid", axis=2, tiled=True),
        lax.all_gather(cotangent, "hid", axis=2, tiled=True),
    )
    inputs = inputs[0]
    upstream = upstream[0]
    gate_full, up_full = (
        lax.all_gather(gate_weight, "cand", axis=0, tiled=True),
        lax.all_gather(up_weight, "cand", axis=0, tiled=True),
    )
    down_full = lax.all_gather(down_weight, "cand", axis=1, tiled=True)
    width = gate_weight.shape[1]
    places = jnp.arange(block_order.shape[0], dtype=jnp.int32)
    logical = jnp.sum(jnp.where(places == lax.axis_index("hid"), block_order, 0))
    active = logical * width < width_steps[0] * (FF // 8)
    keep = active.astype(jnp.float32)
    gate = jnp.dot(inputs, gate_full, preferred_element_type=jnp.float32)
    up = jnp.dot(inputs, up_full, preferred_element_type=jnp.float32)
    sig = jax.nn.sigmoid(gate)
    act = keep * gate * sig
    hidden = (act * up).astype(jnp.bfloat16)
    dhid = keep * jnp.einsum("td,fd->tf", upstream, down_full, preferred_element_type=jnp.float32)
    forward_d_up = (dhid * act).astype(jnp.bfloat16)
    forward_d_gate = (dhid * up * keep * sig * (1.0 + gate * (1.0 - sig))).astype(jnp.bfloat16)
    down_local = jnp.einsum("tf,td->fd", hidden, upstream, preferred_element_type=jnp.float32)
    down_local, d_gate, d_up = (down_local, forward_d_gate, forward_d_up)
    gate_local = jnp.einsum("td,tf->df", inputs, d_gate, preferred_element_type=jnp.float32)
    up_local = jnp.einsum("td,tf->df", inputs, d_up, preferred_element_type=jnp.float32)
    input_part = jnp.einsum("tf,df->td", d_gate, gate_full, preferred_element_type=jnp.float32)
    input_part = input_part + jnp.einsum(
        "tf,df->td", d_up, up_full, preferred_element_type=jnp.float32
    )
    gate_local, up_local, input_part = (gate_local, up_local, input_part)
    grad_tokens = lax.psum_scatter(
        input_part[None].astype(jnp.bfloat16), "hid", scatter_dimension=2, tiled=True
    ).astype(jnp.float32)
    grad_gate, grad_up = (
        lax.psum_scatter(
            gate_local.astype(jnp.bfloat16), "cand", scatter_dimension=0, tiled=True
        ).astype(jnp.float32),
        lax.psum_scatter(
            up_local.astype(jnp.bfloat16), "cand", scatter_dimension=0, tiled=True
        ).astype(jnp.float32),
    )
    grad_down = lax.psum_scatter(
        down_local.astype(jnp.bfloat16), "cand", scatter_dimension=1, tiled=True
    ).astype(jnp.float32)
    return (grad_tokens, grad_gate, grad_up, grad_down)


def solution(mesh):
    in_specs = (
        P("cand", None, "hid"),
        P("cand", None, "hid"),
        P("cand", "hid"),
        P("cand", "hid"),
        P("hid", "cand"),
        P("cand"),
        P(),
    )
    out_specs = (P("cand", None, "hid"), P("cand", "hid"), P("cand", "hid"), P("hid", "cand"))
    return jax.shard_map(shards, mesh=mesh, in_specs=in_specs, out_specs=out_specs, check_vma=False)
```

profile of v0, /device:TPU:1, one launch (start us, length us, event | category | flops | bytes accessed | tf_op | source)
XLA Modules:
  0.0 421.5 jit_solution(7583610765798703201)
XLA Ops:
  7.2 0.0 all-gather.10.cloned.1.call-start
  7.2 0.7 all-gather.10.cloned.1.call-update
  7.9 0.0 all-gather.12.cloned.1.call-start
  7.9 0.7 all-gather.12.cloned.1.call-update
  8.6 0.0 all-gather.14.cloned.1.call-start
  8.7 0.7 all-gather.14.cloned.1.call-update
  9.4 0.0 all-gather.6.cloned.1.call-start
  9.4 0.5 all-gather.6.cloned.1.call-update
  10.0 0.0 all-gather.8.cloned.1.call-start
  10.0 0.5 all-gather.8.cloned.1.call-update
  10.5 0.0 reduce-scatter.5.cloned.1.call-start
  11.2 1.3 fusion.10
  13.2 35.8 %all-gather.10.cloned.1.call-done = bf16[1,256,2048]{2,1,0:T(8,128)(2,1)} async-done(((bf16[1,256,256]{2,1,0:T(8,128)(2,1)}), bf16[1,256,2048]{2,1,0:T(8,128)(2,1)}) %all-gather.10.cloned.1.call-update) | async-done | bytes 1048592 | tf_op jit(solution)/shard_map/all_gather | solution.py:11
  49.0 0.0 copy-start
  49.0 37.9 %all-gather.12.cloned.1.call-done = bf16[2048,1024]{1,0:T(8,128)(2,1)} async-done(((bf16[512,1024]{1,0:T(8,128)(2,1)}), bf16[2048,1024]{1,0:T(8,128)(2,1)}) %all-gather.12.cloned.1.call-update) | async-done | bytes 4194320 | tf_op jit(solution)/shard_map/all_gather | solution.py:18
  87.0 3.8 fusion.6
  90.7 0.0 copy-start.4
  90.8 32.3 %all-gather.14.cloned.1.call-done = bf16[2048,1024]{1,0:T(8,128)(2,1)} async-done(((bf16[512,1024]{1,0:T(8,128)(2,1)}), bf16[2048,1024]{1,0:T(8,128)(2,1)}) %all-gather.14.cloned.1.call-update) | async-done | bytes 4194320 | tf_op jit(solution)/shard_map/all_gather | solution.py:17
  123.0 0.0 copy-done
  123.0 4.4 %fusion.4 = f32[256,1024]{1,0:T(8,128)} fusion(bf16[2048,1024]{1,0:T(8,128)(2,1)} %all-gather.14.cloned.1.call-done, bf16[1,256,2048]{2,1,0:T(8,128)(2,1)S(1)} %copy-done), kind=kOutput, calls=%fused_computation.9 | convolution fusion | flops 1073741824 | bytes 6291456 | tf_op jit(solution)/shard_map/dot_general | solution.py:26
  127.4 34.0 %all-gather.6.cloned.1.call-done = bf16[1,256,2048]{2,1,0:T(8,128)(2,1)} async-done(((bf16[1,256,256]{2,1,0:T(8,128)(2,1)}), bf16[1,256,2048]{2,1,0:T(8,128)(2,1)}) %all-gather.6.cloned.1.call-update) | async-done | bytes 1048592 | tf_op jit(solution)/shard_map/all_gather | solution.py:12
  161.5 37.8 %all-gather.8.cloned.1.call-done = bf16[1024,2048]{1,0:T(8,128)(2,1)} async-done(((bf16[1024,512]{1,0:T(8,128)(2,1)}), bf16[1024,2048]{1,0:T(8,128)(2,1)}) %all-gather.8.cloned.1.call-update) | async-done | bytes 4194320 | tf_op jit(solution)/shard_map/all_gather | solution.py:20
  199.3 0.0 copy-start.2
  199.3 4.6 %multiply_convert_fusion.1 = (bf16[256,1024]{1,0:T(8,128)(2,1)S(1)}, bf16[256,1024]{1,0:T(8,128)(2,1)S(1)}) fusion(f32[256,1024]{1,0:T(8,128)} %fusion.4, f32[]{:T(128)S(6)} %convert_element_type.45, f32[256,1024]{1,0:T(8,128)S(1)} %fusion.6, bf16[1024,2048]{1,0:T(8,128)(2,1)} %all-gather.8.cloned.1.call-done, ...), kind=kOutput, calls=%fused_computation.16 | convolution fusion | flops 1077936128 | bytes 8388612 | tf_op jit(solution)/shard_map/td,fd->tf/dot_general | solution.py:31
  203.9 0.0 copy-done.4
  203.9 0.0 copy-start.1
  203.9 0.0 copy-done.2
  203.9 1.3 fusion.12
  205.2 0.9 copy-done.1
  206.1 0.0 copy-start.3
  206.1 2.3 fusion.1
  208.3 0.0 reduce-scatter.5.cloned.1.call-update
  208.4 0.0 reduce-scatter.11.cloned.1.call-start
  208.4 0.0 copy-done.3
  208.4 4.9 %convolution_convert_fusion = bf16[1024,2048]{1,0:T(8,128)(2,1)} fusion(bf16[1,256,2048]{2,1,0:T(8,128)(2,1)S(1)} %copy-done.3, f32[256,1024]{1,0:T(8,128)} %copy-done.4, f32[256,1024]{1,0:T(8,128)} %fusion.4, f32[]{:T(128)S(6)} %convert_element_type.45), kind=kOutput, calls=%fused_computation.2 | convolution fusion | flops 1077673984 | bytes 7340036 | tf_op jit(solution)/shard_map/tf,td->fd/dot_general | solution.py:34
  213.3 0.0 reduce-scatter.11.cloned.1.call-update
  213.3 0.0 reduce-scatter.9.cloned.1.call-start
  213.4 3.3 convert_bitcast_fusion
  216.6 0.0 reduce-scatter.9.cloned.1.call-update
  216.7 0.0 reduce-scatter.7.cloned.1.call-start
  216.7 3.3 convert_bitcast_fusion.1
  220.0 0.0 reduce-scatter.7.cloned.1.call-update
  220.0 50.9 %reduce-scatter.5.cloned.1.call-done = bf16[1,256,256]{2,1,0:T(8,128)(2,1)} async-done(((bf16[1,256,2048]{2,1,0:T(8,128)(2,1)}), bf16[1,256,256]{2,1,0:T(8,128)(2,1)}) %reduce-scatter.5.cloned.1.call-update) | async-done | bytes 131088 | tf_op jit(solution)/shard_map/reduce_scatter | solution.py:43
  270.9 1.6 convert_element_type.50
  272.5 45.9 %reduce-scatter.11.cloned.1.call-done = bf16[1024,512]{1,0:T(8,128)(2,1)} async-done(((bf16[1024,2048]{1,0:T(8,128)(2,1)}), bf16[1024,512]{1,0:T(8,128)(2,1)}) %reduce-scatter.11.cloned.1.call-update) | async-done | bytes 1048592 | tf_op jit(solution)/shard_map/reduce_scatter | solution.py:54
  318.4 2.8 convert_element_type.59
  321.3 44.1 %reduce-scatter.9.cloned.1.call-done = bf16[512,1024]{0,1:T(8,128)(2,1)} async-done(((bf16[2048,1024]{0,1:T(8,128)(2,1)}), bf16[512,1024]{0,1:T(8,128)(2,1)}) %reduce-scatter.9.cloned.1.call-update) | async-done | bytes 1048592 | tf_op jit(solution)/shard_map/reduce_scatter | solution.py:50
  365.4 2.6 copy.12
  368.0 44.4 %reduce-scatter.7.cloned.1.call-done = bf16[512,1024]{0,1:T(8,128)(2,1)} async-done(((bf16[2048,1024]{0,1:T(8,128)(2,1)}), bf16[512,1024]{0,1:T(8,128)(2,1)}) %reduce-scatter.7.cloned.1.call-update) | async-done | bytes 1048592 | tf_op jit(solution)/shard_map/reduce_scatter | solution.py:47
  412.4 2.6 copy.11
Async XLA Ops:
  7.2 41.9 %all-gather.10.cloned.1.call-start = ((), (), s32[]{:S(2)}) async-start(), calls=%async_computation.6 | async-start | bytes 1179648 | tf_op jit(solution)/shard_map/all_gather | solution.py:11
  7.9 79.1 %all-gather.12.cloned.1.call-start = ((), (), s32[]{:S(2)}) async-start(), calls=%async_computation.7 | async-start | bytes 5242880 | tf_op jit(solution)/shard_map/all_gather | solution.py:18
  8.6 114.4 %all-gather.14.cloned.1.call-start = ((), (), s32[]{:S(2)}) async-start(), calls=%async_computation.8 | async-start | bytes 5242880 | tf_op jit(solution)/shard_map/all_gather | solution.py:17
  9.4 152.1 %all-gather.6.cloned.1.call-start = ((), (), s32[]{:S(2)}) async-start(), calls=%async_computation.4 | async-start | bytes 1179648 | tf_op jit(solution)/shard_map/all_gather | solution.py:12
  10.0 189.3 %all-gather.8.cloned.1.call-start = ((), (), s32[]{:S(2)}) async-start(), calls=%async_computation.5 | async-start | bytes 5242880 | tf_op jit(solution)/shard_map/all_gather | solution.py:20
  10.5 260.3 %reduce-scatter.5.cloned.1.call-start = ((), (), s32[]{:S(2)}) async-start(), calls=%async_computation.9 | async-start | bytes 1179648 | tf_op jit(solution)/shard_map/reduce_scatter | solution.py:43
  49.0 74.0 %copy-start = (bf16[1,256,2048]{2,1,0:T(8,128)(2,1)S(1)}, bf16[1,256,2048]{2,1,0:T(8,128)(2,1)}, u32[]{:S(2)}) copy-start(bf16[1,256,2048]{2,1,0:T(8,128)(2,1)} %all-gather.10.cloned.1.call-done) | copy-start | bytes 3145732
  90.7 113.1 %copy-start.4 = (f32[256,1024]{1,0:T(8,128)}, f32[256,1024]{1,0:T(8,128)S(1)}, u32[]{:S(2)}) copy-start(f32[256,1024]{1,0:T(8,128)S(1)} %fusion.6) | copy-start | bytes 3145732
  199.3 4.6 %copy-start.2 = (bf16[2048,1024]{1,0:T(8,128)(2,1)S(1)}, bf16[2048,1024]{1,0:T(8,128)(2,1)}, u32[]{:S(2)}) copy-start(bf16[2048,1024]{1,0:T(8,128)(2,1)} %all-gather.14.cloned.1.call-done) | copy-start | bytes 12582916
  203.9 2.2 copy-start.1
  206.1 2.3 copy-start.3
  208.4 110.1 %reduce-scatter.11.cloned.1.call-start = ((), (), s32[]{:S(2)}) async-start(), calls=%async_computation.12 | async-start | bytes 5242880 | tf_op jit(solution)/shard_map/reduce_scatter | solution.py:54
  213.3 152.1 %reduce-scatter.9.cloned.1.call-start = ((), (), s32[]{:S(2)}) async-start(), calls=%async_computation.11 | async-start | bytes 5242880 | tf_op jit(solution)/shard_map/reduce_scatter | solution.py:50
  216.7 195.7 %reduce-scatter.7.cloned.1.call-start = ((), (), s32[]{:S(2)}) async-start(), calls=%async_computation.10 | async-start | bytes 5242880 | tf_op jit(solution)/shard_map/reduce_scatter | solution.py:47
Sparse Core Ops, SparseCore 0:
  10.0 38.9 all-gather.9
  50.6 36.3 all-gather.11
  88.5 34.4 all-gather.13
  124.9 36.4 all-gather.5
  162.9 36.3 all-gather.7
  208.5 62.3 reduce-scatter.4
  273.4 44.9 reduce-scatter.10
  321.0 44.3 reduce-scatter.8
  367.9 44.3 reduce-scatter.6
where the time goes:
time: 423 us; the launch traced here: 421 us
  waiting for transfers between devices  366 us (87%)
  matrix products  27.7 us (7%)
  between operations  15.2 us (4%)
  local copies, waits for them, and re-layouts  6.02 us (1%)
  other arithmetic  5.75 us (1%)
    reduce_scatter x1, waiting for transfers between devices, shards(): lax.psum_scatter(input_part[None].astype(jnp.bfloat16), 'hid', scatter_di...  50.9 us
    reduce_scatter x1, waiting for transfers between devices, shards(): lax.psum_scatter(down_local.astype(jnp.bfloat16), 'cand', scatter_dimensi...  45.9 us
    reduce_scatter x1, waiting for transfers between devices, shards(): lax.psum_scatter(gate_local.astype(jnp.bfloat16), 'cand', scatter_dimensi...  44.4 us
    reduce_scatter x1, waiting for transfers between devices, shards(): lax.psum_scatter(up_local.astype(jnp.bfloat16), 'cand', scatter_dimension...  44.1 us
    all_gather x1, waiting for transfers between devices, shards(): lax.all_gather(up_weight, 'cand', axis=0, tiled=True)  37.9 us
    all_gather x1, waiting for transfers between devices, shards(): down_full = lax.all_gather(down_weight, 'cand', axis=1, tiled=True)  37.8 us
    all_gather x1, waiting for transfers between devices, shards(): lax.all_gather(tokens, 'hid', axis=2, tiled=True)  35.8 us
    all_gather x1, waiting for transfers between devices, shards(): lax.all_gather(cotangent, 'hid', axis=2, tiled=True)  34 us
  transfers between devices with their start and end apart: 9, of which 9 were waited for; matrix products, arithmetic and copies ran while one was open for 7% of the time, Pallas kernels for 0%

commit v1 on v0

v1 whole, which is shorter than its diff:
```python
import functools

import jax
import jax.numpy as jnp
from jax import lax
from jax.experimental import pallas as pl
from jax.experimental.pallas import tpu as pltpu
from jax.sharding import PartitionSpec as P

F32, BF16 = jnp.float32, jnp.bfloat16
MESH = pl.DeviceIdType.MESH


def mm(a, b, ca, cb):
    return lax.dot_general(a, b, (((ca,), (cb,)), ((), ())), preferred_element_type=F32)


def kernel(
    nc, nh, keep_ref, tok_ref, cot_ref, gw_ref, uw_ref, dw_ref,
    gt_ref, gg_ref, gu_ref, gd_ref,
    xs, kbuf, psend, prcv, pown, ysend, yrcv, dbuf, accg, accu, accd, part, parr,
    lsem, s1s, s1r, xup, xdn, xcs, xr, ks, kr, ps, pr, ys, yr, ds, dr, qs, qr,
):
    c, h = lax.axis_index("cand"), lax.axis_index("hid")
    per = nh // nc
    rows = nh // per
    row, col = h // per, h % per
    groups = nc // 2
    grp, core = c // 2, c % 2
    sib = grp * 2 + 1 - core
    toks, dh = tok_ref.shape[1], tok_ref.shape[2]
    half = gw_ref.shape[1] // 2
    mine = pl.ds(pl.multiple_of(core * half, half), half)
    other = pl.ds(pl.multiple_of((1 - core) * half, half), half)

    def rcopy(src, dst, ssem, rsem, to):
        return pltpu.make_async_remote_copy(
            src_ref=src, dst_ref=dst, send_sem=ssem, recv_sem=rsem, device_id=to, device_id_type=MESH
        )

    barrier = pltpu.get_barrier_semaphore()

    @pl.loop(0, nh)
    def _(i):
        @pl.when(i != h)
        def _():
            pl.semaphore_signal(barrier, inc=1, device_id=(c, i), device_id_type=MESH)

        @pl.when((row != c) | (i != h))
        def _():
            pl.semaphore_signal(barrier, inc=1, device_id=(row, i), device_id_type=MESH)

    @pl.loop(0, nc)
    def _(i):
        @pl.when(i != c)
        def _():
            pl.semaphore_signal(barrier, inc=1, device_id=(i, h), device_id_type=MESH)

    own = jnp.where(row == c, 1, 0)
    pl.semaphore_wait(barrier, (nh - 1) + (nc - 1) + nh - own)

    def first(a, s):
        ref = (tok_ref, cot_ref)[a].at[0]
        return rcopy(ref, xs.at[s, col, a], s1s.at[a], s1r.at[s, a], (row, h))

    locals_ = [
        pltpu.make_async_copy(ref.at[0], xs.at[c, col, a], lsem.at[a])
        for a, ref in enumerate((tok_ref, cot_ref))
    ]

    @pl.when(row == c)
    def _():
        for cp in locals_:
            cp.start()

    @pl.when(row != c)
    def _():
        for a in range(2):
            first(a, c).start()

    def keep_copy(j):
        to = lax.rem(c + j, nc)
        return rcopy(keep_ref, kbuf.at[j], ks.at[j], kr.at[j], (to, h))

    for j in range(1, nc):
        keep_copy(j).start()
    kbuf[0] = keep_ref[...]

    accg[...] = jnp.zeros_like(accg)
    accu[...] = jnp.zeros_like(accu)
    accd[...] = jnp.zeros_like(accd)

    @pl.when(row == c)
    def _():
        for cp in locals_:
            cp.wait()

    def up_copy(s):
        return rcopy(xs.at[s, col], xs.at[s, col], xup.at[s], xr.at[s, col], (c, h + per))

    def down_copy(s):
        return rcopy(xs.at[s, col], xs.at[s, col], xdn.at[s], xr.at[s, col], (c, h - per))

    def col_copy(s, j):
        to = lax.rem(col + j, per)
        return rcopy(xs.at[s, col], xs.at[s, col], xcs.at[s, j], xr.at[s, col], (c, row * per + to))

    goes_up = (row >= c) & (row < rows - 1)
    goes_down = (row <= c) & (row > 0)

    def pass_on(s):
        @pl.when((row == c) & (s != c))
        def _():
            for a in range(2):
                first(a, s).wait_recv()

        @pl.when(row != c)
        def _():
            rcopy(xs.at[s, col], xs.at[s, col], xup.at[s], xr.at[s, col], (c, h)).wait_recv()

        @pl.when(goes_up)
        def _():
            up_copy(s).start()

        @pl.when(goes_down)
        def _():
            down_copy(s).start()

        for j in range(1, per):
            col_copy(s, j).start()

    def gathered(s, a):
        return jnp.concatenate([xs[s, i, a] for i in range(per)], axis=-1)

    def p_copy(s, a):
        return rcopy(psend.at[s, a], prcv.at[s, a], ps.at[s, a], pr.at[s, a], (sib, h))

    def y_copy(s, a, j):
        to = lax.rem(grp + j, groups) * 2 + core
        return rcopy(ysend.at[s, a], yrcv.at[j - 1, s, a], ys.at[j - 1, s, a], yr.at[j - 1, s, a], (to, h))

    def d_copy(s):
        return rcopy(dbuf.at[s, core], dbuf.at[s, core], ds.at[s], dr.at[s], (sib, h))

    def products(s, where):
        yield 0, mm(gathered(s, 0), gw_ref[:, where], 1, 0)
        yield 1, mm(gathered(s, 0), uw_ref[:, where], 1, 0)
        yield 2, mm(gathered(s, 1), dw_ref[where, :], 1, 1)

    @pl.loop(0, nc + 1)
    def _(t):
        @pl.when(t < nc)
        def _():
            pass_on(t)

        @pl.when(t >= 1)
        def _():
            s = t - 1
            for j in range(1, per):
                oc = lax.rem(col + j, per)
                rcopy(xs.at[s, oc], xs.at[s, oc], xcs.at[s, j], xr.at[s, oc], (c, h)).wait_recv()
            for a, p in products(s, other):
                psend[s, a] = p.astype(BF16)
                p_copy(s, a).start()
            for a, p in products(s, mine):
                pown[s, a] = p
            for a in range(3):
                p_copy(s, a).wait_recv()

                @pl.loop(0, toks // 64)
                def _(i):
                    at = pl.ds(pl.multiple_of(i * 64, 64), 64)
                    both = pown[s, a, at, :] + prcv[s, a, at, :].astype(F32)
                    pown[s, a, at, :] = both
                    ysend[s, a, at, :] = both.astype(BF16)

                for j in range(1, groups):
                    y_copy(s, a, j).start()

    for j in range(1, nc):
        keep_copy(j).wait()

    def part_copy(s, i):
        return rcopy(part.at[s, i], parr.at[h], qs.at[s, i], qr.at[h], (s, c * per + i))

    def stays(s, i):
        return (s == c) & (h == c * per + i)

    @pl.loop(0, nc)
    def _(s):
        for a in range(3):
            for j in range(1, groups):
                y_copy(s, a, j).wait_recv()
        keep = kbuf[lax.rem(c - s + nc, nc), 0:1, 0:1]

        @pl.loop(0, toks // 16)
        def _(i):
            at = pl.ds(pl.multiple_of(i * 16, 16), 16)
            total = [pown[s, a, at, :] for a in range(3)]
            for j in range(groups - 1):
                total = [total[a] + yrcv[j, s, a, at, :].astype(F32) for a in range(3)]
            gate, up, dhid = total
            sig = jax.nn.sigmoid(gate)
            act = keep * gate * sig
            dhid = keep * dhid
            dbuf[s, core, 0, at, :] = (act * up).astype(BF16)
            dbuf[s, core, 1, at, :] = (dhid * act).astype(BF16)
            dbuf[s, core, 2, at, :] = (dhid * up * keep * sig * (1.0 + gate * (1.0 - sig))).astype(BF16)

        d_copy(s).start()
        rcopy(dbuf.at[s, 1 - core], dbuf.at[s, 1 - core], ds.at[s], dr.at[s], (sib, h)).wait_recv()

        for i in range(per):
            at = slice(i * dh, (i + 1) * dh)
            piece = sum(
                mm(dbuf[s, k, a], w[at, k * half:(k + 1) * half], 1, 1)
                for k in range(2)
                for a, w in ((2, gw_ref), (1, uw_ref))
            )
            part[s, i] = piece.astype(BF16)

            @pl.when(stays(s, i))
            def _():
                cp = pltpu.make_async_copy(part.at[s, i], parr.at[h], lsem.at[0])
                cp.start()
                cp.wait()

            @pl.when(jnp.logical_not(stays(s, i)))
            def _():
                part_copy(s, i).start()

        for k in range(2):
            at = slice(k * half, (k + 1) * half)
            accg[:, at] += mm(gathered(s, 0), dbuf[s, k, 2], 0, 0)
            accu[:, at] += mm(gathered(s, 0), dbuf[s, k, 1], 0, 0)
            accd[at, :] += mm(dbuf[s, k, 0], gathered(s, 1), 0, 0)

    gg_ref[...] = accg[...].astype(BF16)
    gu_ref[...] = accu[...].astype(BF16)
    gd_ref[...] = accd[...].astype(BF16)

    for i in range(nh):
        @pl.when((row != c) | (h != i))
        def _():
            rcopy(parr.at[i], parr.at[i], qs.at[0, 0], qr.at[i], (c, h)).wait_recv()

    gt_ref[0] = sum(parr[i].astype(F32) for i in range(nh))

    @pl.when(row != c)
    def _():
        for a in range(2):
            first(a, c).wait_send()

    @pl.loop(0, nc)
    def _(s):
        @pl.when(goes_up)
        def _():
            up_copy(s).wait_send()

        @pl.when(goes_down)
        def _():
            down_copy(s).wait_send()

        for j in range(1, per):
            col_copy(s, j).wait_send()
        for a in range(3):
            p_copy(s, a).wait_send()
            for j in range(1, groups):
                y_copy(s, a, j).wait_send()
        d_copy(s).wait_send()
        for i in range(per):
            @pl.when(jnp.logical_not(stays(s, i)))
            def _():
                part_copy(s, i).wait_send()


def shards(nc, nh, tokens, cotangent, gate_weight, up_weight, down_weight, width_steps, block_order):
    width = gate_weight.shape[1]
    ff = width * nh
    places = jnp.arange(nh, dtype=jnp.int32)
    logical = jnp.sum(jnp.where(places == lax.axis_index("hid"), block_order, 0))
    active = logical * width < width_steps[0] * (ff // 8)
    keep = jnp.broadcast_to(active.astype(F32), (8, 128))
    toks, dh = tokens.shape[1:]
    dq, half = gate_weight.shape[0], width // 2
    per, groups = nh // nc, nc // 2
    sem = pltpu.SemaphoreType.DMA
    vm = pltpu.VMEM
    vspec = pl.BlockSpec(memory_space=pltpu.VMEM)
    out = jax.ShapeDtypeStruct
    gt, gg, gu, gd = pl.pallas_call(
        functools.partial(kernel, nc, nh),
        out_shape=(
            out((1, toks, dh), F32), out((dq, width), BF16), out((dq, width), BF16), out((width, dq), BF16),
        ),
        in_specs=[vspec] * 6,
        out_specs=(vspec,) * 4,
        scratch_shapes=[
            vm((nc, per, 2, toks, dh), BF16),
            vm((nc, 8, 128), F32),
            vm((nc, 3, toks, half), BF16),
            vm((nc, 3, toks, half), BF16),
            vm((nc, 3, toks, half), F32),
            vm((nc, 3, toks, half), BF16),
            vm((groups - 1, nc, 3, toks, half), BF16),
            vm((nc, 2, 3, toks, half), BF16),
            vm((dq, width), F32),
            vm((dq, width), F32),
            vm((width, dq), F32),
            vm((nc, per, toks, dh), BF16),
            vm((nh, toks, dh), BF16),
            sem((2,)), sem((2,)), sem((nc, 2)), sem((nc,)), sem((nc,)), sem((nc, per)), sem((nc, per)),
            sem((nc,)), sem((nc,)), sem((nc, 3)), sem((nc, 3)),
            sem((groups - 1, nc, 3)), sem((groups - 1, nc, 3)), sem((nc,)), sem((nc,)),
            sem((nc, per)), sem((nh,)),
        ],
        compiler_params=pltpu.CompilerParams(
            collective_id=0, has_side_effects=True, vmem_limit_bytes=67043328
        ),
    )(keep, tokens, cotangent, gate_weight, up_weight, down_weight)
    return gt, gg.astype(F32), gu.astype(F32), gd.astype(F32)


def solution(mesh):
    in_specs = (
        P("cand", None, "hid"),
        P("cand", None, "hid"),
        P("cand", "hid"),
        P("cand", "hid"),
        P("hid", "cand"),
        P("cand"),
        P(),
    )
    out_specs = (P("cand", None, "hid"), P("cand", "hid"), P("cand", "hid"), P("hid", "cand"))
    body = functools.partial(shards, mesh.shape["cand"], mesh.shape["hid"])
    return jax.shard_map(body, mesh=mesh, in_specs=in_specs, out_specs=out_specs, check_vma=False)
```

time: 423 us -> 145 us (0.34)
  the two profiles are of different devices: /device:TPU:1 before, /device:TPU:7 now
where the time goes in v1:
time: 145 us
  Pallas kernels  134 us (92%)
  other arithmetic  7.35 us (5%)
  between operations  1.96 us (1%)
    pallas_call x1, Pallas kernels, shards(): pl.pallas_call(functools.partial(kernel, nc, nh), out_shape=(out((1, toks...  134 us
    convert_element_type x3, other arithmetic, shards(): return (gt, gg.astype(F32), gu.astype(F32), gd.astype(F32))  6.05 us

profile of v1, /device:TPU:7, one launch (start us, length us, event | category | flops | bytes accessed | tf_op | source)
XLA Modules:
  0.0 144.6 jit_solution(12290272512543824537)
XLA Ops:
  1.3 1.3 fusion
  3.2 0.6 broadcast_in_dim.8.keep_ref
  3.8 134.0 %shard_map.102 = (f32[1,256,256]{2,1,0:T(8,128)}, bf16[512,1024]{1,0:T(8,128)(2,1)}, bf16[512,1024]{1,0:T(8,128)(2,1)}, bf16[1024,512]{1,0:T(8,128)(2,1)}) custom-call(f32[8,128]{1,0:T(8,128)} %broadcast_in_dim.8.keep_ref, bf16[1,256,256]{2,1,0:T(8,128)(2,1)} %tok_ref.1, bf16[1,256,256]{2,1,0:T(8,128)(2,1)} %cot_ref.1, bf16[512,1024]{1,0:T(8,128)(2,1)} %gw_ref.1, ...), custom_call_target="tpu_custom_call" | custom-call | tf_op jit(solution)/shard_map/pallas_call | solution.py:291
  137.8 0.0 copy-start.1
  137.8 2.9 %convert_element_type.13 = f32[512,1024]{1,0:T(8,128)} convert(bf16[512,1024]{1,0:T(8,128)(2,1)} %get-tuple-element.9) | non-fusion elementwise | flops 524288 | bytes 3145728 | tf_op jit(solution)/shard_map/convert_element_type | solution.py:321
  140.7 0.0 copy-done.1
  140.7 0.0 copy-start
  140.7 1.6 %convert_element_type.14 = f32[512,1024]{1,0:T(8,128)} convert(bf16[512,1024]{1,0:T(8,128)(2,1)S(1)} %copy-done.1) | non-fusion elementwise | flops 524288 | bytes 3145728 | tf_op jit(solution)/shard_map/convert_element_type | solution.py:321
  142.3 0.0 copy-done
  142.3 0.0 copy-start.2
  142.3 1.6 %convert_element_type.15 = f32[1024,512]{1,0:T(8,128)} convert(bf16[1024,512]{1,0:T(8,128)(2,1)S(1)} %copy-done) | non-fusion elementwise | flops 524288 | bytes 3145728 | tf_op jit(solution)/shard_map/convert_element_type | solution.py:321
  143.9 0.0 copy-done.2
  143.9 0.7 copy.13
Async XLA Ops:
  137.8 2.9 %copy-start.1 = (bf16[512,1024]{1,0:T(8,128)(2,1)S(1)}, bf16[512,1024]{1,0:T(8,128)(2,1)}, u32[]{:S(2)}) copy-start(bf16[512,1024]{1,0:T(8,128)(2,1)} %get-tuple-element.10) | copy-start | bytes 3145732
  140.7 1.6 %copy-start = (bf16[1024,512]{1,0:T(8,128)(2,1)S(1)}, bf16[1024,512]{1,0:T(8,128)(2,1)}, u32[]{:S(2)}) copy-start(bf16[1024,512]{1,0:T(8,128)(2,1)} %get-tuple-element.11) | copy-start | bytes 3145732
  142.3 1.6 %copy-start.2 = (f32[1,256,256]{2,1,0:T(8,128)S(1)}, f32[1,256,256]{2,1,0:T(8,128)}, u32[]{:S(2)}) copy-start(f32[1,256,256]{2,1,0:T(8,128)} %get-tuple-element.16) | copy-start | bytes 786436

commit v2 on v1

v2 whole, which is shorter than its diff:
```python
import functools

import jax
import jax.numpy as jnp
from jax import lax
from jax.experimental import pallas as pl
from jax.experimental.pallas import tpu as pltpu
from jax.sharding import PartitionSpec as P

F32, BF16 = jnp.float32, jnp.bfloat16
MESH = pl.DeviceIdType.MESH


def mm(a, b, ca, cb):
    return lax.dot_general(a, b, (((ca,), (cb,)), ((), ())), preferred_element_type=F32)


def kernel(
    nc, nh, ns, slots, ws_ref, bo_ref, tok_ref, cot_ref, gw_hbm, uw_hbm, dw_hbm,
    gt_ref, gg_ref, gu_ref, gd_ref,
    gw_ref, uw_ref, dw_ref, kown, xs, kbuf, psend, prcv, pown, ysend, yrcv, dbuf, accg, accu, accd,
    part, rbuf, red, fin,
    wsem, lsem, s1s, s1r, xup, xdn, xcs, xr, ks, kr, ps, pr, ys, yr, ds, dr, qs, qr, fs, fr, cred,
):
    c, h = lax.axis_index("cand"), lax.axis_index("hid")
    per = nh // nc
    rows = nh // per
    row, col = h // per, h % per
    groups = nc // 2
    grp, core = c // 2, c % 2
    sib = grp * 2 + 1 - core
    toks, dh = tok_ref.shape[1], tok_ref.shape[2]
    tk = toks // ns
    nk = nc * ns
    width = gw_ref.shape[1]
    half = width // 2
    mine = pl.ds(pl.multiple_of(core * half, half), half)
    other = pl.ds(pl.multiple_of((1 - core) * half, half), half)

    def rcopy(src, dst, ssem, rsem, to):
        return pltpu.make_async_remote_copy(
            src_ref=src, dst_ref=dst, send_sem=ssem, recv_sem=rsem, device_id=to, device_id_type=MESH
        )

    loads = [
        pltpu.make_async_copy(src, dst, wsem.at[a])
        for a, (src, dst) in enumerate(((gw_hbm, gw_ref), (uw_hbm, uw_ref), (dw_hbm, dw_ref)))
    ]

    barrier = pltpu.get_barrier_semaphore()

    @pl.loop(0, nh)
    def _(i):
        @pl.when(i != h)
        def _():
            pl.semaphore_signal(barrier, inc=1, device_id=(c, i), device_id_type=MESH)

    @pl.loop(0, nc)
    def _(i):
        @pl.when(i != c)
        def _():
            pl.semaphore_signal(barrier, inc=1, device_id=(i, h), device_id_type=MESH)

    def local(t):
        a, f = t // ns, t % ns
        ref = (tok_ref, cot_ref)[a].at[0, f * tk:(f + 1) * tk]
        return pltpu.make_async_copy(ref, xs.at[c * ns + f, col, a], lsem.at[t])

    @pl.when(row == c)
    def _():
        for t in range(2 * ns):
            local(t).start()

    for cp in loads:
        cp.start()
    level = bo_ref[h] * width - ws_ref[0] * (width * nh // 8)
    kown[...] = jnp.where(jnp.full(kown.shape, level, jnp.int32) < 0, 1.0, 0.0).astype(F32)
    kbuf[0] = kown[...]

    pl.semaphore_wait(barrier, (nh - 1) + (nc - 1))

    def first(a, f, s):
        ref = (tok_ref, cot_ref)[a].at[0, f * tk:(f + 1) * tk]
        k = s * ns + f
        return rcopy(ref, xs.at[k, col, a], s1s.at[f, a], s1r.at[k, a], (row, h))

    @pl.when(row != c)
    def _():
        for f in range(ns):
            for a in range(2):
                first(a, f, c).start()

    def keep_copy(j):
        to = lax.rem(c + j, nc)
        return rcopy(kown, kbuf.at[j], ks.at[j], kr.at[j], (to, h))

    accg[...] = jnp.zeros_like(accg)
    accu[...] = jnp.zeros_like(accu)
    accd[...] = jnp.zeros_like(accd)

    @pl.when(row == c)
    def _():
        for t in range(2 * ns):
            local(t).wait()

    for cp in loads:
        cp.wait()

    def up_copy(k):
        return rcopy(xs.at[k, col], xs.at[k, col], xup.at[k], xr.at[k, col], (c, h + per))

    def down_copy(k):
        return rcopy(xs.at[k, col], xs.at[k, col], xdn.at[k], xr.at[k, col], (c, h - per))

    def col_copy(k, j):
        to = lax.rem(col + j, per)
        return rcopy(xs.at[k, col], xs.at[k, col], xcs.at[k, j], xr.at[k, col], (c, row * per + to))

    goes_up = (row >= c) & (row < rows - 1)
    goes_down = (row <= c) & (row > 0)

    def pass_on(k):
        s = k // ns

        @pl.when((row == c) & (s != c))
        def _():
            for a in range(2):
                rcopy(xs.at[k, col, a], xs.at[k, col, a], s1s.at[0, a], s1r.at[k, a], (c, h)).wait_recv()

        @pl.when(row != c)
        def _():
            rcopy(xs.at[k, col], xs.at[k, col], xup.at[k], xr.at[k, col], (c, h)).wait_recv()

        @pl.when(goes_up)
        def _():
            up_copy(k).start()

        @pl.when(goes_down)
        def _():
            down_copy(k).start()

        for j in range(1, per):
            col_copy(k, j).start()

    def gathered(k, a):
        return jnp.concatenate([xs[k, i, a] for i in range(per)], axis=-1)

    def gathered_all(s, a):
        return jnp.concatenate([gathered(s * ns + f, a) for f in range(ns)], axis=0)

    def p_copy(k, a):
        return rcopy(psend.at[k, a], prcv.at[k, a], ps.at[k, a], pr.at[k, a], (sib, h))

    def y_copy(k, a, j):
        to = lax.rem(grp + j, groups) * 2 + core
        return rcopy(ysend.at[k, a], yrcv.at[j - 1, k, a], ys.at[j - 1, k, a], yr.at[j - 1, k, a], (to, h))

    def products(k, where):
        yield 0, mm(gathered(k, 0), gw_ref[:, where], 1, 0)
        yield 1, mm(gathered(k, 0), uw_ref[:, where], 1, 0)
        yield 2, mm(gathered(k, 1), dw_ref[where, :], 1, 1)

    def chunk(t, lead):
        return lax.rem(lead * 2 * ns + t, nk)

    @pl.loop(0, nk + 1)
    def _(t):
        @pl.when(t < nk)
        def _():
            pass_on(chunk(t, grp))

        @pl.when(t >= 1)
        def _():
            k = chunk(t - 1, grp)
            for j in range(1, per):
                oc = lax.rem(col + j, per)
                rcopy(xs.at[k, oc], xs.at[k, oc], xcs.at[k, j], xr.at[k, oc], (c, h)).wait_recv()
            for a, p in products(k, other):
                psend[k, a] = p.astype(BF16)
                p_copy(k, a).start()
            for a, p in products(k, mine):
                pown[k, a] = p
            for a in range(3):
                p_copy(k, a).wait_recv()

                @pl.loop(0, tk // 32)
                def _(i):
                    at = pl.ds(pl.multiple_of(i * 32, 32), 32)
                    both = pown[k, a, at, :] + prcv[k, a, at, :].astype(F32)
                    pown[k, a, at, :] = both
                    ysend[k, a, at, :] = both.astype(BF16)

                for j in range(1, groups):
                    y_copy(k, a, j).start()

    for j in range(1, nc):
        keep_copy(j).start()
    for j in range(1, nc):
        keep_copy(j).wait()

    def d_rows(k):
        return k // ns, pl.ds(pl.multiple_of(lax.rem(k, ns) * tk, tk), tk)

    def d_copy(k, who):
        s, at = d_rows(k)
        ref = dbuf.at[s, who, :, at]
        return rcopy(ref, ref, ds.at[k], dr.at[k], (sib, h))

    def part_copy(t, k, i):
        at = lax.rem(t, slots)
        return rcopy(part.at[k, i], rbuf.at[at, h], qs.at[k, i], qr.at[at, h], (c, c * per + i))

    def stays(i):
        return h == c * per + i

    def fin_copy(k):
        f = lax.rem(k, ns)
        return rcopy(red.at[k], fin.at[f], fs.at[k], fr.at[f], (k // ns, h))

    def collect(t):
        k, at = chunk(t, nxt), lax.rem(t, slots)

        @pl.when(row == c)
        def _():
            @pl.loop(0, nh)
            def _(i):
                @pl.when(i != h)
                def _():
                    rcopy(rbuf.at[at, i], rbuf.at[at, i], qs.at[k, 0], qr.at[at, i], (c, h)).wait_recv()

            red[k] = sum(rbuf[at, i].astype(F32) for i in range(nh)).astype(BF16)

            if slots < nk:
                @pl.loop(0, nh)
                def _(i):
                    @pl.when((i != h) & (t < nk - slots))
                    def _():
                        pl.semaphore_signal(cred.at[col], inc=1, device_id=(c, i), device_id_type=MESH)

            @pl.when(k // ns == c)
            def _():
                fin[lax.rem(k, ns)] = red[k]

            @pl.when(k // ns != c)
            def _():
                fin_copy(k).start()

    lag = 2
    nxt = lax.rem(grp + 1, groups)

    @pl.loop(0, nk)
    def _(t):
        k = chunk(t, nxt)
        s, half_rows = d_rows(k)
        for a in range(3):
            for j in range(1, groups):
                y_copy(k, a, j).wait_recv()
        keep = kbuf[lax.rem(c - s + nc, nc), 0:1, 0:1]

        @pl.loop(0, tk // 16)
        def _(i):
            at = pl.ds(pl.multiple_of(i * 16, 16), 16)
            to = pl.ds(pl.multiple_of(lax.rem(k, ns) * tk + i * 16, 16), 16)
            total = [pown[k, a, at, :] for a in range(3)]
            for j in range(groups - 1):
                total = [total[a] + yrcv[j, k, a, at, :].astype(F32) for a in range(3)]
            gate, up, dhid = total
            sig = jax.nn.sigmoid(gate)
            act = keep * gate * sig
            dhid = keep * dhid
            dbuf[s, core, 0, to, :] = (act * up).astype(BF16)
            dbuf[s, core, 1, to, :] = (dhid * act).astype(BF16)
            dbuf[s, core, 2, to, :] = (dhid * up * keep * sig * (1.0 + gate * (1.0 - sig))).astype(BF16)

        d_copy(k, core).start()
        d_copy(k, 1 - core).wait_recv()

        for i in range(per):
            at = slice(i * dh, (i + 1) * dh)
            piece = sum(
                mm(dbuf[s, b, a, half_rows, :], w[at, b * half:(b + 1) * half], 1, 1)
                for b in range(2)
                for a, w in ((2, gw_ref), (1, uw_ref))
            ).astype(BF16)

            @pl.when(stays(i))
            def _():
                rbuf[lax.rem(t, slots), h] = piece

            @pl.when(jnp.logical_not(stays(i)))
            def _():
                part[k, i] = piece
                if slots < nk:
                    @pl.when(t >= slots)
                    def _():
                        pl.semaphore_wait(cred.at[i], 1)

                part_copy(t, k, i).start()

        @pl.when(t >= lag)
        def _():
            collect(t - lag)

        @pl.when(lax.rem(t, ns) == ns - 1)
        def _():
            for b in range(2):
                at = slice(b * half, (b + 1) * half)
                accg[:, at] += mm(gathered_all(s, 0), dbuf[s, b, 2], 0, 0)
                accu[:, at] += mm(gathered_all(s, 0), dbuf[s, b, 1], 0, 0)
                accd[at, :] += mm(dbuf[s, b, 0], gathered_all(s, 1), 0, 0)

    for t in range(nk - lag, nk):
        collect(jnp.int32(t))

    gg_ref[...] = accg[...].astype(BF16)
    gu_ref[...] = accu[...].astype(BF16)
    gd_ref[...] = accd[...].astype(BF16)

    for f in range(ns):
        @pl.when(row != c)
        def _():
            rcopy(fin.at[f], fin.at[f], fs.at[0], fr.at[f], (c, h)).wait_recv()

        gt_ref[0, f * tk:(f + 1) * tk] = fin[f].astype(F32)

    @pl.when(row != c)
    def _():
        for f in range(ns):
            for a in range(2):
                first(a, f, c).wait_send()

    @pl.loop(0, nk)
    def _(k):
        @pl.when(goes_up)
        def _():
            up_copy(k).wait_send()

        @pl.when(goes_down)
        def _():
            down_copy(k).wait_send()

        for j in range(1, per):
            col_copy(k, j).wait_send()
        for a in range(3):
            p_copy(k, a).wait_send()
            for j in range(1, groups):
                y_copy(k, a, j).wait_send()
        d_copy(k, core).wait_send()
        for i in range(per):
            @pl.when(jnp.logical_not(stays(i)))
            def _():
                part_copy(k, k, i).wait_send()

        @pl.when((row == c) & (k // ns != c))
        def _():
            fin_copy(k).wait_send()


def shards(nc, nh, tokens, cotangent, gate_weight, up_weight, down_weight, width_steps, block_order):
    width = gate_weight.shape[1]
    toks, dh = tokens.shape[1:]
    dq, half = gate_weight.shape[0], width // 2
    per, groups = nh // nc, nc // 2
    ns = 2
    nk, tk = nc * ns, toks // ns
    slots = min(nk, (8 << 20) // (nh * tk * max(dh, 128) * 2))
    sem = pltpu.SemaphoreType.DMA
    vm = pltpu.VMEM
    vspec = pl.BlockSpec(memory_space=pltpu.VMEM)
    sspec = pl.BlockSpec(memory_space=pltpu.SMEM)
    anyspec = pl.BlockSpec(memory_space=pl.ANY)
    out = jax.ShapeDtypeStruct
    gt, gg, gu, gd = pl.pallas_call(
        functools.partial(kernel, nc, nh, ns, slots),
        out_shape=(
            out((1, toks, dh), F32), out((dq, width), BF16), out((dq, width), BF16), out((width, dq), BF16),
        ),
        in_specs=[sspec] * 2 + [anyspec] * 5,
        out_specs=(vspec,) * 4,
        scratch_shapes=[
            vm((dq, width), BF16),
            vm((dq, width), BF16),
            vm((width, dq), BF16),
            vm((8, 128), F32),
            vm((nk, per, 2, tk, dh), BF16),
            vm((nc, 8, 128), F32),
            vm((nk, 3, tk, half), BF16),
            vm((nk, 3, tk, half), BF16),
            vm((nk, 3, tk, half), F32),
            vm((nk, 3, tk, half), BF16),
            vm((groups - 1, nk, 3, tk, half), BF16),
            vm((nc, 2, 3, toks, half), BF16),
            vm((dq, width), F32),
            vm((dq, width), F32),
            vm((width, dq), F32),
            vm((nk, per, tk, dh), BF16),
            vm((slots, nh, tk, dh), BF16),
            vm((nk, tk, dh), BF16),
            vm((ns, tk, dh), BF16),
            sem((3,)), sem((2 * ns,)), sem((ns, 2)), sem((nk, 2)), sem((nk,)), sem((nk,)), sem((nk, per)),
            sem((nk, per)), sem((nc,)), sem((nc,)), sem((nk, 3)), sem((nk, 3)),
            sem((groups - 1, nk, 3)), sem((groups - 1, nk, 3)), sem((nk,)), sem((nk,)),
            sem((nk, per)), sem((slots, nh)), sem((nk,)), sem((ns,)), pltpu.SemaphoreType.REGULAR((per,)),
        ],
        compiler_params=pltpu.CompilerParams(
            collective_id=0, has_side_effects=True, vmem_limit_bytes=67043328
        ),
    )(width_steps, block_order, tokens, cotangent, gate_weight, up_weight, down_weight)
    return gt, gg.astype(F32), gu.astype(F32), gd.astype(F32)


def solution(mesh):
    in_specs = (
        P("cand", None, "hid"),
        P("cand", None, "hid"),
        P("cand", "hid"),
        P("cand", "hid"),
        P("hid", "cand"),
        P("cand"),
        P(),
    )
    out_specs = (P("cand", None, "hid"), P("cand", "hid"), P("cand", "hid"), P("hid", "cand"))
    body = functools.partial(shards, mesh.shape["cand"], mesh.shape["hid"])
    return jax.shard_map(body, mesh=mesh, in_specs=in_specs, out_specs=out_specs, check_vma=False)
```

time: 145 us -> 153 us (1.055)
  the two profiles are of different devices: /device:TPU:7 before, /device:TPU:1 now
where the time goes in v2:
time: 153 us
  Pallas kernels  145 us (95%)
  other arithmetic  6.05 us (4%)
    pallas_call x1, Pallas kernels, shards(): pl.pallas_call(functools.partial(kernel, nc, nh, ns, slots), out_shape=(o...  145 us
    convert_element_type x3, other arithmetic, shards(): return (gt, gg.astype(F32), gu.astype(F32), gd.astype(F32))  6.05 us

profile of v2, /device:TPU:1, one launch (start us, length us, event | category | flops | bytes accessed | tf_op | source)
XLA Modules:
  0.0 152.6 jit_solution(12641412453914185034)
XLA Ops:
  1.3 144.6 %shard_map.102 = (f32[1,256,256]{2,1,0:T(8,128)}, bf16[512,1024]{1,0:T(8,128)(2,1)}, bf16[512,1024]{1,0:T(8,128)(2,1)}, bf16[1024,512]{1,0:T(8,128)(2,1)}) custom-call(s32[1]{0:T(128)S(6)} %copy.12.ws_ref, s32[8]{0:T(128)} %bo_ref.1, bf16[1,256,256]{2,1,0:T(8,128)(2,1)} %tok_ref.1, bf16[1,256,256]{2,1,0:T(8,128)(2,1)} %cot_ref.1, bf16[512,1024]{1,0:T(8,128)(2,1)} %gw_hbm.1, ...), custom_call_target="tpu_custom_call" | custom-call | tf_op jit(solution)/shard_map/pallas_call | solution.py:373
  145.8 0.0 copy-start.1
  145.8 2.9 %convert_element_type.9 = f32[512,1024]{1,0:T(8,128)} convert(bf16[512,1024]{1,0:T(8,128)(2,1)} %get-tuple-element.9) | non-fusion elementwise | flops 524288 | bytes 3145728 | tf_op jit(solution)/shard_map/convert_element_type | solution.py:409
  148.7 0.0 copy-done.1
  148.7 0.0 copy-start
  148.7 1.6 %convert_element_type.10 = f32[512,1024]{1,0:T(8,128)} convert(bf16[512,1024]{1,0:T(8,128)(2,1)S(1)} %copy-done.1) | non-fusion elementwise | flops 524288 | bytes 3145728 | tf_op jit(solution)/shard_map/convert_element_type | solution.py:409
  150.3 0.0 copy-done
  150.3 0.0 copy-start.2
  150.3 1.6 %convert_element_type.11 = f32[1024,512]{1,0:T(8,128)} convert(bf16[1024,512]{1,0:T(8,128)(2,1)S(1)} %copy-done) | non-fusion elementwise | flops 524288 | bytes 3145728 | tf_op jit(solution)/shard_map/convert_element_type | solution.py:409
  151.9 0.0 copy-done.2
  151.9 0.7 copy.13
Async XLA Ops:
  145.8 2.9 %copy-start.1 = (bf16[512,1024]{1,0:T(8,128)(2,1)S(1)}, bf16[512,1024]{1,0:T(8,128)(2,1)}, u32[]{:S(2)}) copy-start(bf16[512,1024]{1,0:T(8,128)(2,1)} %get-tuple-element.10) | copy-start | bytes 3145732
  148.7 1.6 %copy-start = (bf16[1024,512]{1,0:T(8,128)(2,1)S(1)}, bf16[1024,512]{1,0:T(8,128)(2,1)}, u32[]{:S(2)}) copy-start(bf16[1024,512]{1,0:T(8,128)(2,1)} %get-tuple-element.11) | copy-start | bytes 3145732
  150.3 1.6 %copy-start.2 = (f32[1,256,256]{2,1,0:T(8,128)S(1)}, f32[1,256,256]{2,1,0:T(8,128)}, u32[]{:S(2)}) copy-start(f32[1,256,256]{2,1,0:T(8,128)} %get-tuple-element.16) | copy-start | bytes 786436

commit v3 on v1

--- a/solution.py
+++ b/solution.py
@@ -16,9 +16,9 @@
 
 
 def kernel(
-    nc, nh, keep_ref, tok_ref, cot_ref, gw_ref, uw_ref, dw_ref,
+    nc, nh, ws_ref, bo_ref, tok_ref, cot_ref, gw_hbm, uw_hbm, dw_hbm,
     gt_ref, gg_ref, gu_ref, gd_ref,
-    xs, kbuf, psend, prcv, pown, ysend, yrcv, dbuf, accg, accu, accd, part, parr,
+    gw_ref, uw_ref, dw_ref, keep_ref, wsem, xs, kbuf, psend, prcv, pown, ysend, yrcv, dbuf, accg, accu, accd, part, parr,
     lsem, s1s, s1r, xup, xdn, xcs, xr, ks, kr, ps, pr, ys, yr, ds, dr, qs, qr,
 ):
     c, h = lax.axis_index("cand"), lax.axis_index("hid")
@@ -38,6 +38,16 @@
             src_ref=src, dst_ref=dst, send_sem=ssem, recv_sem=rsem, device_id=to, device_id_type=MESH
         )
 
+    loads = [
+        pltpu.make_async_copy(src, dst, wsem.at[a])
+        for a, (src, dst) in enumerate(((gw_hbm, gw_ref), (uw_hbm, uw_ref), (dw_hbm, dw_ref)))
+    ]
+    for cp in loads:
+        cp.start()
+    width = gw_ref.shape[1]
+    level = bo_ref[h] * width - ws_ref[0] * (width * nh // 8)
+    keep_ref[...] = jnp.where(jnp.full(keep_ref.shape, level, jnp.int32) < 0, 1.0, 0.0).astype(F32)
+
     barrier = pltpu.get_barrier_semaphore()
 
     @pl.loop(0, nh)
@@ -89,6 +99,8 @@
     accg[...] = jnp.zeros_like(accg)
     accu[...] = jnp.zeros_like(accu)
     accd[...] = jnp.zeros_like(accd)
+    for cp in loads:
+        cp.wait()
 
     @pl.when(row == c)
     def _():
@@ -151,11 +163,11 @@
     def _(t):
         @pl.when(t < nc)
         def _():
-            pass_on(t)
+            pass_on(lax.rem(grp * 2 + t, nc))
 
         @pl.when(t >= 1)
         def _():
-            s = t - 1
+            s = lax.rem(grp * 2 + t - 1, nc)
             for j in range(1, per):
                 oc = lax.rem(col + j, per)
                 rcopy(xs.at[s, oc], xs.at[s, oc], xcs.at[s, j], xr.at[s, oc], (c, h)).wait_recv()
@@ -186,8 +198,11 @@
     def stays(s, i):
         return (s == c) & (h == c * per + i)
 
+    nxt = lax.rem(grp + 1, groups)
+
     @pl.loop(0, nc)
-    def _(s):
+    def _(t):
+        s = lax.rem(nxt * 2 + t, nc)
         for a in range(3):
             for j in range(1, groups):
                 y_copy(s, a, j).wait_recv()
@@ -276,11 +291,6 @@
 
 def shards(nc, nh, tokens, cotangent, gate_weight, up_weight, down_weight, width_steps, block_order):
     width = gate_weight.shape[1]
-    ff = width * nh
-    places = jnp.arange(nh, dtype=jnp.int32)
-    logical = jnp.sum(jnp.where(places == lax.axis_index("hid"), block_order, 0))
-    active = logical * width < width_steps[0] * (ff // 8)
-    keep = jnp.broadcast_to(active.astype(F32), (8, 128))
     toks, dh = tokens.shape[1:]
     dq, half = gate_weight.shape[0], width // 2
     per, groups = nh // nc, nc // 2
@@ -293,9 +303,10 @@
         out_shape=(
             out((1, toks, dh), F32), out((dq, width), BF16), out((dq, width), BF16), out((width, dq), BF16),
         ),
-        in_specs=[vspec] * 6,
+        in_specs=[pl.BlockSpec(memory_space=pltpu.SMEM)] * 2 + [pl.BlockSpec(memory_space=pl.ANY)] * 5,
         out_specs=(vspec,) * 4,
         scratch_shapes=[
+            vm((dq, width), BF16), vm((dq, width), BF16), vm((width, dq), BF16), vm((8, 128), F32), sem((3,)),
             vm((nc, per, 2, toks, dh), BF16),
             vm((nc, 8, 128), F32),
             vm((nc, 3, toks, half), BF16),
@@ -317,7 +328,7 @@
         compiler_params=pltpu.CompilerParams(
             collective_id=0, has_side_effects=True, vmem_limit_bytes=67043328
         ),
-    )(keep, tokens, cotangent, gate_weight, up_weight, down_weight)
+    )(width_steps, block_order, tokens, cotangent, gate_weight, up_weight, down_weight)
     return gt, gg.astype(F32), gu.astype(F32), gd.astype(F32)
 
 

time: 145 us -> 135 us (0.931)
  the two profiles are of different devices: /device:TPU:7 before, /device:TPU:1 now
where the time goes in v3:
time: 135 us; the launch traced here: 134 us
  Pallas kernels  126 us (93%)
  other arithmetic  6.05 us (4%)
    pallas_call x1, Pallas kernels, shards(): pl.pallas_call(functools.partial(kernel, nc, nh), out_shape=(out((1, toks...  126 us
    convert_element_type x3, other arithmetic, shards(): return (gt, gg.astype(F32), gu.astype(F32), gd.astype(F32))  6.05 us

profile of v3, /device:TPU:1, one launch (start us, length us, event | category | flops | bytes accessed | tf_op | source)
XLA Modules:
  0.0 133.7 jit_solution(11163025058517344779)
XLA Ops:
  1.3 125.6 %shard_map.102 = (f32[1,256,256]{2,1,0:T(8,128)}, bf16[512,1024]{1,0:T(8,128)(2,1)}, bf16[512,1024]{1,0:T(8,128)(2,1)}, bf16[1024,512]{1,0:T(8,128)(2,1)}) custom-call(s32[1]{0:T(128)S(6)} %copy.12.ws_ref, s32[8]{0:T(128)} %bo_ref.1, bf16[1,256,256]{2,1,0:T(8,128)(2,1)} %tok_ref.1, bf16[1,256,256]{2,1,0:T(8,128)(2,1)} %cot_ref.1, bf16[512,1024]{1,0:T(8,128)(2,1)} %gw_hbm.1, ...), custom_call_target="tpu_custom_call" | custom-call | tf_op jit(solution)/shard_map/pallas_call | solution.py:301
  126.9 0.0 copy-start.1
  126.9 2.9 %convert_element_type.9 = f32[512,1024]{1,0:T(8,128)} convert(bf16[512,1024]{1,0:T(8,128)(2,1)} %get-tuple-element.9) | non-fusion elementwise | flops 524288 | bytes 3145728 | tf_op jit(solution)/shard_map/convert_element_type | solution.py:332
  129.8 0.0 copy-done.1
  129.8 0.0 copy-start
  129.8 1.6 %convert_element_type.10 = f32[512,1024]{1,0:T(8,128)} convert(bf16[512,1024]{1,0:T(8,128)(2,1)S(1)} %copy-done.1) | non-fusion elementwise | flops 524288 | bytes 3145728 | tf_op jit(solution)/shard_map/convert_element_type | solution.py:332
  131.4 0.0 copy-done
  131.4 0.0 copy-start.2
  131.4 1.6 %convert_element_type.11 = f32[1024,512]{1,0:T(8,128)} convert(bf16[1024,512]{1,0:T(8,128)(2,1)S(1)} %copy-done) | non-fusion elementwise | flops 524288 | bytes 3145728 | tf_op jit(solution)/shard_map/convert_element_type | solution.py:332
  133.0 0.0 copy-done.2
  133.0 0.7 copy.13
Async XLA Ops:
  126.9 2.9 %copy-start.1 = (bf16[512,1024]{1,0:T(8,128)(2,1)S(1)}, bf16[512,1024]{1,0:T(8,128)(2,1)}, u32[]{:S(2)}) copy-start(bf16[512,1024]{1,0:T(8,128)(2,1)} %get-tuple-element.10) | copy-start | bytes 3145732
  129.8 1.6 %copy-start = (bf16[1024,512]{1,0:T(8,128)(2,1)S(1)}, bf16[1024,512]{1,0:T(8,128)(2,1)}, u32[]{:S(2)}) copy-start(bf16[1024,512]{1,0:T(8,128)(2,1)} %get-tuple-element.11) | copy-start | bytes 3145732
  131.4 1.6 %copy-start.2 = (f32[1,256,256]{2,1,0:T(8,128)S(1)}, f32[1,256,256]{2,1,0:T(8,128)}, u32[]{:S(2)}) copy-start(f32[1,256,256]{2,1,0:T(8,128)} %get-tuple-element.16) | copy-start | bytes 786436
